TPU v7x, 128 devices: a whole 4x4x4 slice. The times are simulated.
128 devices in a mesh: vel: 8 (over y, z_lo), space: 16 (over x, z_hi, core).
Axes of the slice: x: 4, y: 4, z: 4 (z_hi: 2, z_lo: 2; z = z_hi * 2 + z_lo), core: 2. Of those that a mesh axis runs over, the one named last changes fastest.
Arguments:
- density: float32 [1024, 64, 8, 128], P('vel', 'space'), may hold values from -6 to 6
- limiter: int32 [64, 8, 128], P('space'), may hold values from 0 to 2
- heading: int32 [1024], P('vel'), may hold values from 0 to 1
- courant: float32 [1024], P('vel'), may hold values from 0.1 to 0.9
- kernel_slices: bfloat16 [16, 1024, 1024], P('space', None, 'vel'), may hold values from -0.046875 to 0.046875
Outputs:
- transported: float32 [1024, 64, 8, 128], P('vel', 'space')
- collision: float32 [1024, 64, 8, 128], P('vel', 'space')
Inputs may be any that keep to these rules, and one draw needn't show every extreme that they name: `limiter`: 0 no slope, 1 minmod slope, 2 central slope.
All inputs are finite; a program needn't handle non-finite values.
Results may differ from a plain program's by a relative error of at most 0.0041.
Values may be sent and summed in bfloat16 or wider, within the bound.
No kernel may reach another device: no remote copies, remote signals or barrier semaphores. Data moves between devices by JAX's collectives and lax.ppermute only.
A program may use at most 128 MiB of HBM per device.

v0:
```python
import jax
import jax.numpy as jnp
from jax import lax
from jax.sharding import PartitionSpec as P

V = 1024
SLICES = 16


def extended(shard, sides, width):
    for axis, dim in sides:
        size, length = (lax.axis_size(axis), shard.shape[dim])
        up = [(i, (i + 1) % size) for i in range(size - 1)]
        down = [(j, i) for i, j in up]
        last = lax.slice_in_dim(shard, length - width, length, axis=dim)
        first = lax.slice_in_dim(shard, 0, width, axis=dim)
        before = lax.ppermute(last, axis, up)
        after = lax.ppermute(first, axis, down)
        shard = jnp.concatenate([before, shard, after], axis=dim)
    return shard


def limited_slopes(left_diff, right_diff, limiter):
    minmod_slope = jnp.where(
        left_diff * right_diff > 0,
        jnp.sign(left_diff) * jnp.minimum(jnp.abs(left_diff), jnp.abs(right_diff)),
        jnp.zeros_like(left_diff),
    )
    central = 0.5 * (left_diff + right_diff)
    codes = limiter[None]
    return jnp.where(
        codes == 1, minmod_slope, jnp.where(codes == 2, central, jnp.zeros_like(central))
    )


def make_fold(source, totals, pieces):
    stride = V // SLICES

    def one_slice(counter, running):
        matrix = lax.dynamic_index_in_dim(pieces, counter, 0, keepdims=False)
        projected = lax.dot_general(
            matrix, source, (((0,), (0,)), ((), ())), preferred_element_type=jnp.float32
        )
        weight = lax.dynamic_index_in_dim(source, counter * stride, 0, keepdims=True).astype(
            jnp.float32
        )
        return running + weight * projected

    return lax.fori_loop(0, pieces.shape[0], one_slice, totals)


def local(density, limiter, heading, courant, kernel_slices):
    padded = extended(density, (("space", 1),), 1)
    left_diff = density - padded[:, :-2]
    right_diff = padded[:, 2:] - density
    slopes = limited_slopes(left_diff, right_diff, limiter)
    upwind = (2 * heading - 1).astype(jnp.float32)[:, None, None, None]
    rebuilt = density + 0.5 * upwind * slopes
    rebuilt_pad = extended(rebuilt, (("space", 1),), 1)
    forward = (heading == 1)[:, None, None, None]
    upstream = jnp.where(forward, rebuilt_pad[:, :-2], rebuilt_pad[:, 2:])
    transported = density - courant[:, None, None, None] * (rebuilt - upstream)
    flattened = transported.astype(jnp.bfloat16).reshape(density.shape[0], -1)
    columns = lax.all_to_all(flattened, "vel", split_axis=1, concat_axis=0, tiled=True)
    full_slices = lax.all_gather(kernel_slices, "vel", axis=2, tiled=True)
    initial = jnp.zeros(columns.shape, jnp.float32)
    summed = make_fold(columns, initial, lax.all_gather(full_slices, "space", axis=0, tiled=True))
    restored = lax.all_to_all(summed, "vel", split_axis=0, concat_axis=1, tiled=True)
    return (transported, restored.reshape(density.shape))


def solution(mesh):
    return jax.shard_map(
        local,
        mesh=mesh,
        in_specs=(
            P("vel", "space", None, None),
            P("space", None, None),
            P("vel"),
            P("vel"),
            P("space", None, "vel"),
        ),
        out_specs=(P("vel", "space", None, None), P("vel", "space", None, None)),
        check_vma=False,
    )
```

profile of v0, /device:TPU:1, one launch (start us, length us, event | category | flops | bytes accessed | tf_op | source)
XLA Modules:
  0.0 379.8 jit_solution(10808552207556664224)
XLA Ops:
  7.9 61.5 %all-gather.3.cloned.1.call-done = bf16[1,1024,1024]{2,1,0:T(8,128)(2,1)} async-done(((bf16[1,1024,128]{2,1,0:T(8,128)(2,1)}), bf16[1,1024,1024]{2,1,0:T(8,128)(2,1)}) %all-gather.3.cloned.1.call-update) | async-done | bytes 2097168 | tf_op jit(solution)/shard_map/all_gather | solution.py:65
  71.6 6.6 %collective-permute-start = (f32[128,1,8,128]{0,3,2,1:T(8,128)S(1)}, f32[128,1,8,128]{0,3,2,1:T(8,128)S(1)}, u32[]{:S(2)}, u32[]{:S(2)}) collective-permute-start(f32[128,1,8,128]{0,3,2,1:T(8,128)S(1)} %get-tuple-element.111), channel_id=1, source_target_pairs={{0,1},{1,2},{2,3},{3,4},{4,5},{5,6},{6,7},{7,8},{8,9},{9,10},{10,1... | collective-permute-start | bytes 1572872 | tf_op jit(solution)/shard_map/ppermute | solution.py:17
  80.2 11.6 %collective-permute-done = f32[128,1,8,128]{0,3,2,1:T(8,128)S(1)} collective-permute-done((f32[128,1,8,128]{0,3,2,1:T(8,128)S(1)}, f32[128,1,8,128]{0,3,2,1:T(8,128)S(1)}, u32[]{:S(2)}, u32[]{:S(2)}) %collective-permute-start) | collective-permute-done | bytes 524320 | tf_op jit(solution)/shard_map/ppermute | solution.py:17
  93.8 5.9 %collective-permute-start.2 = (f32[128,1,8,128]{0,3,2,1:T(8,128)S(1)}, f32[128,1,8,128]{0,3,2,1:T(8,128)S(1)}, u32[]{:S(2)}, u32[]{:S(2)}) collective-permute-start(f32[128,1,8,128]{0,3,2,1:T(8,128)S(1)} %get-tuple-element.109), channel_id=1, source_target_pairs={{0,1},{1,2},{2,3},{3,4},{4,5},{5,6},{6,7},{7,8},{8,9},{9,10},{10,1... | collective-permute-start | bytes 1572872 | tf_op jit(solution)/shard_map/ppermute | solution.py:17
  101.6 26.6 %collective-permute-done.2 = f32[128,1,8,128]{0,3,2,1:T(8,128)S(1)} collective-permute-done((f32[128,1,8,128]{0,3,2,1:T(8,128)S(1)}, f32[128,1,8,128]{0,3,2,1:T(8,128)S(1)}, u32[]{:S(2)}, u32[]{:S(2)}) %collective-permute-start.2) | collective-permute-done | bytes 524320 | tf_op jit(solution)/shard_map/ppermute | solution.py:17
  131.4 3.6 all-to-all-start
  135.0 10.2 %all-to-all-done = bf16[128,8,512]{2,0,1:T(8,128)(2,1)S(1)} async-done(((bf16[128,8,512]{2,0,1:T(8,128)(2,1)}), bf16[128,8,512]{2,0,1:T(8,128)(2,1)S(1)}, u32[]{:S(2)}, u32[]{:S(2)}) %all-to-all-start) | async-done | bytes 1048608 | tf_op jit(solution)/shard_map/all_to_all | solution.py:64
  145.2 135.5 %all-gather.5.cloned.1.call-done = bf16[16,1024,1024]{2,1,0:T(8,128)(2,1)} async-done(((bf16[1,1024,1024]{2,1,0:T(8,128)(2,1)}), bf16[16,1024,1024]{2,1,0:T(8,128)(2,1)}) %all-gather.5.cloned.1.call-update) | async-done | bytes 33554448 | tf_op jit(solution)/shard_map/all_gather | solution.py:67
  280.7 51.4 %while.14 = (s32[]{:T(128)}, f32[1024,512]{1,0:T(8,128)S(1)}, bf16[1024,512]{1,0:T(8,128)(2,1)S(1)}, bf16[16,1024,1024]{2,1,0:T(8,128)(2,1)}, s32[]{:T(128)}, /*index=5*/s32[]{:T(128)}, s32[]{:T(128)}, s32[]{:T(128)}) while((s32[]{:T(128)}, f32[1024,512]{1,0:T(8,128)S(1)}, bf16[1024,512]{1,0:T(8,128)(2,1)S(1)}, ...), condition=%wide.region_1.2_spmd.clone, body=%wide.region_0.1_spmd.clone.sunk | while | flops 1075315200 | bytes 7345809 | solution.py:49
  283.9 3.2 select_add_fusion.2
  287.1 3.2 select_add_fusion.2
  290.4 3.2 select_add_fusion.2
  293.6 3.2 select_add_fusion.2
  296.8 3.2 select_add_fusion.2
  300.0 3.2 select_add_fusion.2
  303.2 3.2 select_add_fusion.2
  306.4 3.2 select_add_fusion.2
  309.7 3.2 select_add_fusion.2
  312.9 3.2 select_add_fusion.2
  316.1 3.2 select_add_fusion.2
  319.3 3.2 select_add_fusion.2
  322.5 3.2 select_add_fusion.2
  333.4 4.5 %all-to-all-start.1 = ((f32[8,128,512]{2,1,0:T(8,128)}), f32[8,128,512]{2,1,0:T(8,128)}, u32[]{:S(2)}, u32[]{:S(2)}) async-start(f32[8,128,512]{2,1,0:T(8,128)} %bitcast.23), calls=%async_computation.1 | async-start | bytes 4194304 | tf_op jit(solution)/shard_map/all_to_all | solution.py:68
  339.9 29.2 %all-to-all-done.1 = f32[8,128,512]{2,1,0:T(8,128)} async-done(((f32[8,128,512]{2,1,0:T(8,128)}), f32[8,128,512]{2,1,0:T(8,128)}, u32[]{:S(2)}, u32[]{:S(2)}) %all-to-all-start.1) | async-done | bytes 2097184 | tf_op jit(solution)/shard_map/all_to_all | solution.py:68
  (50 shorter events, 28.7 us)
Async XLA Ops:
  7.2 62.3 %all-gather.3.cloned.1.call-start = ((), (), s32[]{:S(2)}) async-start(), calls=%async_computation.2 | async-start | bytes 2359296 | tf_op jit(solution)/shard_map/all_gather | solution.py:65
  7.9 272.8 %all-gather.5.cloned.1.call-start = ((), (), s32[]{:S(2)}) async-start(), calls=%async_computation.3 | async-start | bytes 35651584 | tf_op jit(solution)/shard_map/all_gather | solution.py:67
  71.5 8.6 %copy-start.4 = (s32[128]{0:T(128)S(1)}, s32[128]{0:T(128)}, u32[]{:S(2)}) copy-start(s32[128]{0:T(128)} %param.9) | copy-start | bytes 1540
  71.5 8.7 %copy-start.2 = (s32[4,8,128]{2,1,0:T(8,128)S(1)}, s32[4,8,128]{2,1,0:T(8,128)}, u32[]{:S(2)}) copy-start(s32[4,8,128]{2,1,0:T(8,128)} %param.8) | copy-start | bytes 49156
  71.6 20.2 %collective-permute-start = (f32[128,1,8,128]{0,3,2,1:T(8,128)S(1)}, f32[128,1,8,128]{0,3,2,1:T(8,128)S(1)}, u32[]{:S(2)}, u32[]{:S(2)}) collective-permute-start(f32[128,1,8,128]{0,3,2,1:T(8,128)S(1)} %get-tuple-element.111), channel_id=1, source_target_pairs={{0,1},{1,2},{2,3},{3,4},{4,5},{5,6},{6,7},{7,8},{8,9},{9,10},{10,1... | collective-permute-start | bytes 1572872 | tf_op jit(solution)/shard_map/ppermute | solution.py:17
  78.2 13.6 %collective-permute-start.1 = (f32[128,1,8,128]{0,3,2,1:T(8,128)S(1)}, f32[128,1,8,128]{0,3,2,1:T(8,128)S(1)}, u32[]{:S(2)}, u32[]{:S(2)}) collective-permute-start(f32[128,1,8,128]{0,3,2,1:T(8,128)S(1)} %get-tuple-element.112), channel_id=1, source_target_pairs={{1,0},{2,1},{3,2},{4,3},{5,4},{6,5},{7,6},{8,7},{9,8},{10,9},{11,1... | collective-permute-start | bytes 1572872 | tf_op jit(solution)/shard_map/ppermute | solution.py:18
  93.7 34.5 %copy-start.3 = (f32[128]{0:T(128)S(1)}, f32[128]{0:T(128)}, u32[]{:S(2)}) copy-start(f32[128]{0:T(128)} %param.10) | copy-start | bytes 1540
  93.8 34.4 %collective-permute-start.2 = (f32[128,1,8,128]{0,3,2,1:T(8,128)S(1)}, f32[128,1,8,128]{0,3,2,1:T(8,128)S(1)}, u32[]{:S(2)}, u32[]{:S(2)}) collective-permute-start(f32[128,1,8,128]{0,3,2,1:T(8,128)S(1)} %get-tuple-element.109), channel_id=1, source_target_pairs={{0,1},{1,2},{2,3},{3,4},{4,5},{5,6},{6,7},{7,8},{8,9},{9,10},{10,1... | collective-permute-start | bytes 1572872 | tf_op jit(solution)/shard_map/ppermute | solution.py:17
  99.7 28.5 %collective-permute-start.3 = (f32[128,1,8,128]{0,3,2,1:T(8,128)S(1)}, f32[128,1,8,128]{0,3,2,1:T(8,128)S(1)}, u32[]{:S(2)}, u32[]{:S(2)}) collective-permute-start(f32[128,1,8,128]{0,3,2,1:T(8,128)S(1)} %get-tuple-element.110), channel_id=1, source_target_pairs={{1,0},{2,1},{3,2},{4,3},{5,4},{6,5},{7,6},{8,7},{9,8},{10,9},{11,1... | collective-permute-start | bytes 1572872 | tf_op jit(solution)/shard_map/ppermute | solution.py:18
  131.4 13.8 %all-to-all-start = ((bf16[128,8,512]{2,0,1:T(8,128)(2,1)}), bf16[128,8,512]{2,0,1:T(8,128)(2,1)S(1)}, u32[]{:S(2)}, u32[]{:S(2)}) async-start(bf16[128,8,512]{2,0,1:T(8,128)(2,1)} %copy.17), calls=%async_computation | async-start | bytes 2097152 | tf_op jit(solution)/shard_map/all_to_all | solution.py:64
  332.1 1.3 copy-start.1
  333.4 4.5 %copy-start = (f32[128,4,8,128]{0,3,2,1:T(8,128)S(1)}, f32[128,4,8,128]{0,3,2,1:T(8,128)}, u32[]{:S(2)}) copy-start(f32[128,4,8,128]{0,3,2,1:T(8,128)} %get-tuple-element.108) | copy-start | bytes 6291460
  333.4 35.7 %all-to-all-start.1 = ((f32[8,128,512]{2,1,0:T(8,128)}), f32[8,128,512]{2,1,0:T(8,128)}, u32[]{:S(2)}, u32[]{:S(2)}) async-start(f32[8,128,512]{2,1,0:T(8,128)} %bitcast.23), calls=%async_computation.1 | async-start | bytes 4194304 | tf_op jit(solution)/shard_map/all_to_all | solution.py:68
Sparse Core Ops, SparseCore 0:
  9.6 59.8 all-gather.2
  71.8 208.8 all-gather.4
where the time goes:
time: 381 us; the launch traced here: 380 us
  waiting for transfers between devices  275 us (72%)
  matrix products  50.7 us (13%)
  starting transfers between devices  24.5 us (6%)
  between operations  14.2 us (4%)
  local copies, waits for them, and re-layouts  10.6 us (3%)
  other arithmetic  3.97 us (1%)
    all_gather x1, waiting for transfers between devices, local(): lax.all_gather(full_slices, 'space', axis=0, tiled=True)  136 us
    all_gather x1, waiting for transfers between devices, local(): full_slices = lax.all_gather(kernel_slices, 'vel', axis=2, tiled=True)  61.5 us
    dot_general x16, matrix products, one_slice(): lax.dot_general(matrix, source, (((0,), (0,)), ((), ())), preferred_eleme...  50.7 us
    ppermute x2, waiting for transfers between devices, extended(): before = lax.ppermute(last, axis, up)  38.2 us
    all_to_all x1, waiting for transfers between devices, local(): lax.all_to_all(summed, 'vel', split_axis=0, concat_axis=1, tiled=True)  29.2 us
    ppermute x2, starting transfers between devices, extended(): before = lax.ppermute(last, axis, up)  12.5 us
    all_to_all x1, waiting for transfers between devices, local(): lax.all_to_all(flattened, 'vel', split_axis=1, concat_axis=0, tiled=True)  10.2 us
  transfers between devices with their start and end apart: 8, of which 6 were waited for; matrix products, arithmetic and copies ran while one was open for 2% of the time, Pallas kernels for 0%

commit v1 on v0

--- a/solution.py
+++ b/solution.py
@@ -1,3 +1,4 @@
+import functools
 import jax
 import jax.numpy as jnp
 from jax import lax
@@ -5,6 +6,18 @@
 
 V = 1024
 SLICES = 16
+
+
+def test_the_strips_all(field_in, ndim_at, array_dim):
+    return jnp.concatenate(
+        lax.all_to_all(
+            jnp.stack(jnp.split(field_in, lax.axis_size("vel"), axis=ndim_at), axis=0), "vel", 0, 0
+        ),
+        axis=array_dim,
+    )
+
+
+connect_threads = functools.partial(test_the_strips_all, ndim_at=1, array_dim=0)
 
 
 def extended(shard, sides, width):
@@ -61,7 +74,7 @@
     upstream = jnp.where(forward, rebuilt_pad[:, :-2], rebuilt_pad[:, 2:])
     transported = density - courant[:, None, None, None] * (rebuilt - upstream)
     flattened = transported.astype(jnp.bfloat16).reshape(density.shape[0], -1)
-    columns = lax.all_to_all(flattened, "vel", split_axis=1, concat_axis=0, tiled=True)
+    columns = connect_threads(flattened)
     full_slices = lax.all_gather(kernel_slices, "vel", axis=2, tiled=True)
     initial = jnp.zeros(columns.shape, jnp.float32)
     summed = make_fold(columns, initial, lax.all_gather(full_slices, "space", axis=0, tiled=True))

time: 381 us -> 375 us (0.984)
  waiting for transfers between devices: 275 us -> 242 us
  blocking collectives: 0 us -> 29.7 us
  starting transfers between devices: 24.5 us -> 20.2 us
    all_to_all x0 -> x1, blocking collectives: none -> 29.7 us  [local(): lax.all_to_all(summed, 'vel', split_axis=0, concat_axis=1, tiled=True)]
    all_to_all x2 -> x1, waiting for transfers between devices: 39.4 us -> 10.1 us  [test_the_strips_all(): lax.all_to_all(jnp.stack(jnp.split(field_in, lax.axis_size('vel'), axis=n...]
    all_to_all x2 -> x1, starting transfers between devices: 8.03 us -> 3.56 us  [test_the_strips_all(): lax.all_to_all(jnp.stack(jnp.split(field_in, lax.axis_size('vel'), axis=n...]
    unnamed x13 -> x19, local copies, waits for them, and re-layouts: 7.26 us -> 9.46 us
  transfers between devices with their start and end apart: 8 -> 7, of which waited for: 6 -> 5; matrix products, arithmetic and copies ran while one was open for 2% -> 3% of each run, Pallas kernels for 0% -> 0%
where the time goes in v1:
time: 375 us; the launch traced here: 374 us
  waiting for transfers between devices  242 us (65%)
  matrix products  50.7 us (14%)
  blocking collectives  29.7 us (8%)
  starting transfers between devices  20.2 us (5%)
  between operations  14.2 us (4%)
  local copies, waits for them, and re-layouts  12.1 us (3%)
  other arithmetic  4.44 us (1%)
    all_gather x1, waiting for transfers between devices, local(): lax.all_gather(full_slices, 'space', axis=0, tiled=True)  133 us
    all_gather x1, waiting for transfers between devices, local(): full_slices = lax.all_gather(kernel_slices, 'vel', axis=2, tiled=True)  61.5 us
    dot_general x16, matrix products, one_slice(): lax.dot_general(matrix, source, (((0,), (0,)), ((), ())), preferred_eleme...  50.7 us
    ppermute x2, waiting for transfers between devices, extended(): before = lax.ppermute(last, axis, up)  36.7 us
    all_to_all x1, blocking collectives, local(): lax.all_to_all(summed, 'vel', split_axis=0, concat_axis=1, tiled=True)  29.7 us
    ppermute x2, starting transfers between devices, extended(): before = lax.ppermute(last, axis, up)  12.8 us
    all_to_all x1, waiting for transfers between devices, test_the_strips_all(): lax.all_to_all(jnp.stack(jnp.split(field_in, lax.axis_size('vel'), axis=n...  10.1 us
    unnamed x19, local copies, waits for them, and re-layouts  9.46 us
  transfers between devices with their start and end apart: 7, of which 5 were waited for; matrix products, arithmetic and copies ran while one was open for 3% of the time, Pallas kernels for 0%

profile of v1, /device:TPU:1, one launch (start us, length us, event | category | flops | bytes accessed | tf_op | source)
XLA Modules:
  0.0 373.6 jit_solution(5773291868022526601)
XLA Ops:
  8.0 61.5 %all-gather.3.cloned.1.call-done = bf16[1,1024,1024]{2,1,0:T(8,128)(2,1)} async-done(((bf16[1,1024,128]{2,1,0:T(8,128)(2,1)}), bf16[1,1024,1024]{2,1,0:T(8,128)(2,1)}) %all-gather.3.cloned.1.call-update) | async-done | bytes 2097168 | tf_op jit(solution)/shard_map/all_gather | solution.py:78
  69.6 6.6 %collective-permute-start = (f32[128,1,8,128]{3,2,1,0:T(8,128)S(1)}, f32[128,1,8,128]{3,2,1,0:T(8,128)S(1)}, u32[]{:S(2)}, u32[]{:S(2)}) collective-permute-start(f32[128,1,8,128]{3,2,1,0:T(8,128)S(1)} %get-tuple-element.111), channel_id=1, source_target_pairs={{0,1},{1,2},{2,3},{3,4},{4,5},{5,6},{6,7},{7,8},{8,9},{9,10},{10,1... | collective-permute-start | bytes 1572872 | tf_op jit(solution)/shard_map/ppermute | solution.py:30
  78.2 10.1 %collective-permute-done = f32[128,1,8,128]{3,2,1,0:T(8,128)S(1)} collective-permute-done((f32[128,1,8,128]{3,2,1,0:T(8,128)S(1)}, f32[128,1,8,128]{3,2,1,0:T(8,128)S(1)}, u32[]{:S(2)}, u32[]{:S(2)}) %collective-permute-start) | collective-permute-done | bytes 524320 | tf_op jit(solution)/shard_map/ppermute | solution.py:30
  90.1 6.2 %collective-permute-start.2 = (f32[128,1,8,128]{3,2,1,0:T(8,128)S(1)}, f32[128,1,8,128]{3,2,1,0:T(8,128)S(1)}, u32[]{:S(2)}, u32[]{:S(2)}) collective-permute-start(f32[128,1,8,128]{3,2,1,0:T(8,128)S(1)} %get-tuple-element.109), channel_id=1, source_target_pairs={{0,1},{1,2},{2,3},{3,4},{4,5},{5,6},{6,7},{7,8},{8,9},{9,10},{10,1... | collective-permute-start | bytes 1572872 | tf_op jit(solution)/shard_map/ppermute | solution.py:30
  98.2 26.6 %collective-permute-done.2 = f32[128,1,8,128]{3,2,1,0:T(8,128)S(1)} collective-permute-done((f32[128,1,8,128]{3,2,1,0:T(8,128)S(1)}, f32[128,1,8,128]{3,2,1,0:T(8,128)S(1)}, u32[]{:S(2)}, u32[]{:S(2)}) %collective-permute-start.2) | collective-permute-done | bytes 524320 | tf_op jit(solution)/shard_map/ppermute | solution.py:30
  133.1 3.6 all-to-all-start
  136.7 10.1 %all-to-all-done = bf16[8,128,512]{2,1,0:T(8,128)(2,1)S(1)} async-done(((bf16[8,128,512]{2,1,0:T(8,128)(2,1)}), bf16[8,128,512]{2,1,0:T(8,128)(2,1)S(1)}, u32[]{:S(2)}, u32[]{:S(2)}) %all-to-all-start) | async-done | bytes 1048608 | tf_op jit(solution)/shard_map/all_to_all | solution.py:13
  146.8 132.6 %all-gather.5.cloned.1.call-done = bf16[16,1024,1024]{2,1,0:T(8,128)(2,1)} async-done(((bf16[1,1024,1024]{2,1,0:T(8,128)(2,1)}), bf16[16,1024,1024]{2,1,0:T(8,128)(2,1)}) %all-gather.5.cloned.1.call-update) | async-done | bytes 33554448 | tf_op jit(solution)/shard_map/all_gather | solution.py:80
  279.4 51.4 %while.14 = (s32[]{:T(128)}, f32[1024,512]{1,0:T(8,128)S(1)}, bf16[1024,512]{1,0:T(8,128)(2,1)S(1)}, bf16[16,1024,1024]{2,1,0:T(8,128)(2,1)}, s32[]{:T(128)}, /*index=5*/s32[]{:T(128)}, s32[]{:T(128)}, s32[]{:T(128)}) while((s32[]{:T(128)}, f32[1024,512]{1,0:T(8,128)S(1)}, bf16[1024,512]{1,0:T(8,128)(2,1)S(1)}, ...), condition=%wide.region_1.2_spmd.clone, body=%wide.region_0.1_spmd.clone.sunk | while | flops 1075315200 | bytes 7345809 | solution.py:62
  282.6 3.2 select_add_fusion.2
  285.9 3.2 select_add_fusion.2
  289.1 3.2 select_add_fusion.2
  292.3 3.2 select_add_fusion.2
  295.5 3.2 select_add_fusion.2
  298.7 3.2 select_add_fusion.2
  302.0 3.2 select_add_fusion.2
  305.2 3.2 select_add_fusion.2
  308.4 3.2 select_add_fusion.2
  311.6 3.2 select_add_fusion.2
  314.8 3.2 select_add_fusion.2
  318.0 3.2 select_add_fusion.2
  321.3 3.2 select_add_fusion.2
  324.5 3.2 select_add_fusion.2
  332.2 29.7 %all_to_all.21 = f32[8,128,512]{2,1,0:T(8,128)S(1)} all-to-all(f32[8,128,512]{2,1,0:T(8,128)} %bitcast.65), channel_id=1, replica_groups=mesh['vel'=8,'space'=16] {'vel'}, dimensions={0} | all-to-all | bytes 4194304 | tf_op jit(solution)/shard_map/all_to_all | solution.py:81
  (55 shorter events, 27.5 us)
Async XLA Ops:
  7.2 62.3 %copy-start = (f32[128,4,8,128]{3,2,1,0:T(8,128)S(1)}, f32[128,4,8,128]{3,2,1,0:T(8,128)}, u32[]{:S(2)}) copy-start(f32[128,4,8,128]{3,2,1,0:T(8,128)} %param.7) | copy-start | bytes 6291460
  7.2 62.3 %all-gather.3.cloned.1.call-start = ((), (), s32[]{:S(2)}) async-start(), calls=%async_computation.2 | async-start | bytes 2359296 | tf_op jit(solution)/shard_map/all_gather | solution.py:78
  7.9 271.5 %all-gather.5.cloned.1.call-start = ((), (), s32[]{:S(2)}) async-start(), calls=%async_computation.3 | async-start | bytes 35651584 | tf_op jit(solution)/shard_map/all_gather | solution.py:80
  69.5 8.7 %copy-start.4 = (s32[128]{0:T(128)S(1)}, s32[128]{0:T(128)}, u32[]{:S(2)}) copy-start(s32[128]{0:T(128)} %param.9) | copy-start | bytes 1540
  69.5 8.7 %copy-start.2 = (s32[4,8,128]{2,1,0:T(8,128)S(1)}, s32[4,8,128]{2,1,0:T(8,128)}, u32[]{:S(2)}) copy-start(s32[4,8,128]{2,1,0:T(8,128)} %param.8) | copy-start | bytes 49156
  69.6 18.7 %collective-permute-start = (f32[128,1,8,128]{3,2,1,0:T(8,128)S(1)}, f32[128,1,8,128]{3,2,1,0:T(8,128)S(1)}, u32[]{:S(2)}, u32[]{:S(2)}) collective-permute-start(f32[128,1,8,128]{3,2,1,0:T(8,128)S(1)} %get-tuple-element.111), channel_id=1, source_target_pairs={{0,1},{1,2},{2,3},{3,4},{4,5},{5,6},{6,7},{7,8},{8,9},{9,10},{10,1... | collective-permute-start | bytes 1572872 | tf_op jit(solution)/shard_map/ppermute | solution.py:30
  76.2 12.1 %collective-permute-start.1 = (f32[128,1,8,128]{3,2,1,0:T(8,128)S(1)}, f32[128,1,8,128]{3,2,1,0:T(8,128)S(1)}, u32[]{:S(2)}, u32[]{:S(2)}) collective-permute-start(f32[128,1,8,128]{3,2,1,0:T(8,128)S(1)} %get-tuple-element.112), channel_id=1, source_target_pairs={{1,0},{2,1},{3,2},{4,3},{5,4},{6,5},{7,6},{8,7},{9,8},{10,9},{11,1... | collective-permute-start | bytes 1572872 | tf_op jit(solution)/shard_map/ppermute | solution.py:31
  90.0 34.8 %copy-start.3 = (f32[128]{0:T(128)S(1)}, f32[128]{0:T(128)}, u32[]{:S(2)}) copy-start(f32[128]{0:T(128)} %param.10) | copy-start | bytes 1540
  90.1 34.7 %collective-permute-start.2 = (f32[128,1,8,128]{3,2,1,0:T(8,128)S(1)}, f32[128,1,8,128]{3,2,1,0:T(8,128)S(1)}, u32[]{:S(2)}, u32[]{:S(2)}) collective-permute-start(f32[128,1,8,128]{3,2,1,0:T(8,128)S(1)} %get-tuple-element.109), channel_id=1, source_target_pairs={{0,1},{1,2},{2,3},{3,4},{4,5},{5,6},{6,7},{7,8},{8,9},{9,10},{10,1... | collective-permute-start | bytes 1572872 | tf_op jit(solution)/shard_map/ppermute | solution.py:30
  96.3 28.5 %collective-permute-start.3 = (f32[128,1,8,128]{3,2,1,0:T(8,128)S(1)}, f32[128,1,8,128]{3,2,1,0:T(8,128)S(1)}, u32[]{:S(2)}, u32[]{:S(2)}) collective-permute-start(f32[128,1,8,128]{3,2,1,0:T(8,128)S(1)} %get-tuple-element.110), channel_id=1, source_target_pairs={{1,0},{2,1},{3,2},{4,3},{5,4},{6,5},{7,6},{8,7},{9,8},{10,9},{11,1... | collective-permute-start | bytes 1572872 | tf_op jit(solution)/shard_map/ppermute | solution.py:31
  133.1 13.7 %all-to-all-start = ((bf16[8,128,512]{2,1,0:T(8,128)(2,1)}), bf16[8,128,512]{2,1,0:T(8,128)(2,1)S(1)}, u32[]{:S(2)}, u32[]{:S(2)}) async-start(bf16[8,128,512]{2,1,0:T(8,128)(2,1)} %fusion.15), calls=%async_computation | async-start | bytes 2097152 | tf_op jit(solution)/shard_map/all_to_all | solution.py:13
  330.9 1.3 copy-start.1
Sparse Core Ops, SparseCore 0:
  9.6 59.8 all-gather.2
  71.9 207.5 all-gather.4
